TPU v7x, 128 devices: a whole 4x4x4 slice. The times are simulated.
128 devices in a mesh: section: 4 (over x), seq: 32 (over z, y, core).
Axes of the slice: x: 4, y: 4, z: 4, core: 2. Of those that a mesh axis runs over, the one named last changes fastest.
Arguments:
- frames_in: bfloat16 [4, 64, 128, 1024], P(None, 'seq'), may hold values from -6 to 6
- order: int32 [4], replicated, may hold values from 0 to 3, each once
- owner: int32 [128], replicated, may hold values from 0 to 31, as said below
- qkv_weight: bfloat16 [4, 1024, 3072], P('section'), may hold values from -1 to 1
- out_weight: bfloat16 [4, 1024, 1024], P('section'), may hold values from -0.1875 to 0.1875
- gains: float32 [4, 1024], P('section'), may hold values from 0.1 to 1.9
Outputs:
- layers_out: bfloat16 [4, 64, 256, 1024], P('section', None, 'seq')
Inputs may be any that keep to these rules, and one draw needn't show every extreme that they name: `owner`: no device owns more than 8 rows, and some device owns exactly 8.
All inputs are finite; a program needn't handle non-finite values.
Results may differ from a plain program's by a relative error of at most 0.02.
Values may be sent and summed in bfloat16 or wider, within the bound.
A program may use at most 128 MiB of HBM per device.

v0:
```python
import functools

import jax
import jax.numpy as jnp
from jax import lax
from jax.experimental import pallas as pl
from jax.experimental.pallas import tpu as pltpu
from jax.sharding import PartitionSpec as P

MESH = pl.DeviceIdType.MESH
HEADS = 16
F32, BF = jnp.float32, jnp.bfloat16


class Gather:
    def __init__(self, wq_in, wo_in, wq, wo, sems):
        self.wq_in, self.wo_in, self.wq, self.wo = wq_in, wo_in, wq, wo
        (self.xs, self.xr, self.p1s, self.p1r, self.p2s, self.p2r) = sems[:6]
        (self.ds, self.dr, self.gs, self.gr, self.es, self.er, self.own) = sems[6:]
        self.x = lax.axis_index("section")
        self.q = lax.axis_index("seq")
        self.c = lax.rem(self.q, 2)
        self.y = lax.rem(self.q // 2, 4)
        self.z = self.q // 8
        self.pending = []

    def dev(self, dx=0, dy=0, dz=0, dc=0):
        x = lax.rem(self.x + (dx + 4), 4)
        y = lax.rem(self.y + (dy + 4), 4)
        z = lax.rem(self.z + (dz + 4), 4)
        c = lax.rem(self.c + dc, 2)
        return (x, (z * 4 + y) * 2 + c)
    def peer(self, k):
        return self.dev(0, lax.rem(k // 2, 4), k // 8, lax.rem(k, 2))

    def source(self, k):
        return self.dev(0, 4 - lax.rem(k // 2, 4), 4 - k // 8, 2 - lax.rem(k, 2))[1]

    def barrier(self):
        sem = pltpu.get_barrier_semaphore()
        for dx in (1, 2, 3):
            pl.semaphore_signal(sem, inc=1, device_id=self.dev(dx=dx), device_id_type=MESH)

        @pl.loop(1, 32)
        def _(k):
            pl.semaphore_signal(sem, inc=1, device_id=self.peer(k), device_id_type=MESH)

        pl.semaphore_wait(sem, 34)

    def copy(self, src, dst, ss, rs, dev):
        return pltpu.make_async_remote_copy(src_ref=src, dst_ref=dst, send_sem=ss, recv_sem=rs, device_id=dev, device_id_type=MESH)
    def send(self, src, dst, ss, rs, dev):
        cp = self.copy(src, dst, ss, rs, dev)
        cp.start()
        self.pending.append(cp)
    def recv(self, dst, ss, rs):
        self.copy(dst, dst, ss, rs, self.dev(dc=1)).wait_recv()
    def rows(self, ab, i=0, blk=0):
        y, z = self.y, self.z
        if ab == 0:
            major, minor = lax.rem(z + (blk + 4), 4), lax.rem(y + (i + 4), 4)
        else:
            major, minor = lax.rem(y + (blk + 4), 4), lax.rem(z + (i + 4), 4)
        return self.c * 512 + ab * 256 + major * 64, minor * 16
    def sl(self, l, ab, i):
        a, b = self.rows(ab, i)
        return self.wq.at[l, pl.ds(pl.multiple_of(a + b, 16), 16), :]
    def slh(self, l, ab, i, h):
        a, b = self.rows(ab, i)
        return self.wq.at[l, pl.ds(pl.multiple_of(a + b, 16), 16), pl.ds(h * 1536, 1536)]
    def blk(self, l, ab, k):
        a, _ = self.rows(ab, 0, k)
        return self.wq.at[l, pl.ds(pl.multiple_of(a, 64), 64), :]
    def blkh(self, l, ab, k, h):
        a, _ = self.rows(ab, 0, k)
        return self.wq.at[l, pl.ds(pl.multiple_of(a + h * 32, 32), 32), :]
    def wop(self, l, h):
        return self.wo.at[l, pl.ds(pl.multiple_of(self.c * 512 + h * 256, 256), 256), :]
    def layer_of(self, d):
        return lax.rem(self.x + d, 4)
    def stage_layer(self, j):
        return j + (self.x <= j).astype(jnp.int32)
    def start_x(self):
        x = self.x
        for ab in (0, 1):
            a, b = self.rows(ab, 0)
            src = self.wq_in.at[0, pl.ds(pl.multiple_of(a + b, 16), 16), :]
            for dx, d in (((1, 3), (-1, 1)) if ab == 0 else ((-1, 1), (1, 3))):
                self.send(src, self.sl(x, ab, 0), self.xs.at[ab, d - 1], self.xr.at[ab, d - 1], self.dev(dx=dx))
    def wo_own(self, second):
        copies = []
        for dx, d, h in ((1, 3, second), (-1, 1, 1 - second)):
            src = self.wo_in.at[0, pl.ds(pl.multiple_of(self.c * 512 + h * 256, 256), 256), :]
            sems = self.xs.at[2 + h, d - 1], self.xr.at[2 + h, d - 1]
            copies.append(self.copy(src, self.wop(self.x, h), *sems, self.dev(dx=dx)))
        return copies

    def wo_first(self):
        for cp in self.wo_own(0):
            cp.start()
            self.pending.append(cp)
        second = self.wo_own(1)
        self.pending.extend(second)

        @pl.when(self.x == 0)
        def _():
            for cp in second:
                cp.start()

    def wo_forward(self):
        for h, d, dx in ((0, 3, 1), (1, 1, -1)):
            r = self.wop(self.layer_of(d), h)
            self.recv(r, self.xs.at[2 + h, d - 1], self.xr.at[2 + h, d - 1])
            self.send(r, r, self.xs.at[2 + h, 1], self.xr.at[2 + h, 1], self.dev(dx=dx))
            self.dd_send(r, 8 + h, d - 1)

        @pl.when(self.x != 0)
        def _():
            for cp in self.wo_own(1):
                cp.start()

    def wo_ready(self, layer):
        dist = lax.rem(layer - self.x + 4, 4)
        for d, hs in ((1, (0,)), (2, (0, 1)), (3, (1,))):
            if layer == 0:
                for h in hs:
                    r = self.wop(self.layer_of(d), h)
                    self.pending.append(
                        self.copy(r, r, self.ds.at[8 + h, d - 1], self.dr.at[8 + h, d - 1], self.dev(dc=1))
                    )

            @pl.when(dist == d)
            def _():
                for h in hs:
                    r = self.wop(self.layer_of(d), h)
                    self.recv(r, self.xs.at[2 + h, d - 1], self.xr.at[2 + h, d - 1])
                    self.copy(r, r, self.ds.at[8 + h, d - 1], self.dr.at[8 + h, d - 1], self.dev(dc=1)).start()
                g = self.other()
                for h in (0, 1):
                    self.recv(g.wop(self.layer_of(d), h), self.ds.at[8 + h, d - 1], self.dr.at[8 + h, d - 1])

    def gains_start(self, g_in, g_all):
        for dx in (1, 2, 3):
            self.send(g_in, g_all.at[self.x], self.gs.at[dx - 1], self.gr.at[dx - 1], self.dev(dx=dx))

    def gains_wait(self, g_all):
        for dx in (1, 2, 3):
            self.recv(g_all.at[self.layer_of(4 - dx)], self.gs.at[dx - 1], self.gr.at[dx - 1])

    def exchange_copy(self, k, send, land):
        src = send.at[pl.ds(pl.multiple_of(self.peer(k)[1] * 16, 16), 16), :]
        dst = land.at[pl.ds(pl.multiple_of(self.q * 16, 16), 16), :]
        return self.copy(src, dst, self.es.at[k], self.er.at[k], self.peer(k))

    def exchange_start(self, send, land):
        @pl.loop(1, 32)
        def _(k):
            self.exchange_copy(k, send, land).start()

        rows = pl.ds(pl.multiple_of(self.q * 16, 16), 16)
        pltpu.make_async_copy(send.at[rows, :], land.at[rows, :], self.es.at[0]).start()

    def exchange_wait(self, send, land):
        @pl.loop(1, 32)
        def _(k):
            rows = pl.ds(pl.multiple_of(self.source(k) * 16, 16), 16)
            self.recv(land.at[rows, :], self.es.at[k], self.er.at[k])

        rows = pl.ds(pl.multiple_of(self.q * 16, 16), 16)
        pltpu.make_async_copy(send.at[rows, :], land.at[rows, :], self.es.at[0]).wait()

    def exchange_drain(self, send, land):
        @pl.loop(1, 32)
        def _(k):
            self.exchange_copy(k, send, land).wait_send()

    def own_copies(self, frames_in, frames, g_in, g_all):
        return [
            pltpu.make_async_copy(frames_in, frames, self.own.at[0]),
            pltpu.make_async_copy(g_in, g_all.at[self.x], self.own.at[1]),
            pltpu.make_async_copy(self.wq_in.at[0], self.wq.at[self.x], self.own.at[2]),
            pltpu.make_async_copy(self.wo_in.at[0], self.wo.at[self.x], self.own.at[3]),
        ]

    def x_forward_qkv(self):
        for ab, d, dx in ((0, 3, 1), (1, 1, -1)):
            l = self.layer_of(d)
            self.recv(self.sl(l, ab, 0), self.xs.at[ab, d - 1], self.xr.at[ab, d - 1])
            self.send(self.sl(l, ab, 0), self.sl(l, ab, 0), self.xs.at[ab, 1], self.xr.at[ab, 1], self.dev(dx=dx))
    def x_wait(self):
        for ab, d in ((0, 1), (1, 3), (0, 2), (1, 2)):
            self.recv(self.sl(self.layer_of(d), ab, 0), self.xs.at[ab, d - 1], self.xr.at[ab, d - 1])
    def dd_send(self, ref, a, b):
        self.send(ref, ref, self.ds.at[a, b], self.dr.at[a, b], self.dev(dc=1))

    def ax(self, phase, ab, s):
        if (phase == 1) == (ab == 0):
            return self.dev(dy=s)
        return self.dev(dz=s)
    def p1s1(self, j):
        l = self.stage_layer(j)
        for n in (0, 1):
            for k, s in enumerate((1, -1)):
                for ab in (0, 1):
                    h = k if n == 0 else 1 - k
                    r = self.slh(l, ab, 0, h)
                    self.send(r, r, self.p1s.at[ab, 2 * n + k, j], self.p1r.at[ab, 2 * n + k, j], self.ax(1, ab, s))
    def p1s2(self, j):
        l = self.stage_layer(j)
        for k, s in enumerate((1, -1)):
            for ab in (0, 1):
                r = self.slh(l, ab, -s, k)
                self.recv(r, self.p1s.at[ab, k, j], self.p1r.at[ab, k, j])
                self.send(r, r, self.p1s.at[ab, 4 + k, j], self.p1r.at[ab, 4 + k, j], self.ax(1, ab, s))
    def p2s1(self, j):
        l = self.stage_layer(j)
        for ab in (0, 1):
            for k, s in enumerate((1, -1)):
                self.recv(self.slh(l, ab, -s, 1 - k), self.p1s.at[ab, 2 + k, j], self.p1r.at[ab, 2 + k, j])
                self.recv(self.slh(l, ab, 2, k), self.p1s.at[ab, 4 + k, j], self.p1r.at[ab, 4 + k, j])
        for n in (0, 1):
            for k, s in enumerate((1, -1)):
                for ab in (0, 1):
                    h = k if n == 0 else 1 - k
                    r = self.blkh(l, ab, 0, h)
                    self.send(r, r, self.p2s.at[ab, 2 * n + k, j], self.p2r.at[ab, 2 * n + k, j], self.ax(2, ab, s))
        for ab in (0, 1):
            self.dd_send(self.blk(l, ab, 0), ab * 4, j)
    def p2s2(self, j):
        l = self.stage_layer(j)
        for k, s in enumerate((1, -1)):
            for ab in (0, 1):
                r = self.blkh(l, ab, -s, k)
                self.recv(r, self.p2s.at[ab, k, j], self.p2r.at[ab, k, j])
                self.send(r, r, self.p2s.at[ab, 4 + k, j], self.p2r.at[ab, 4 + k, j], self.ax(2, ab, s))
    def fin(self, j):
        l = self.stage_layer(j)
        for ab in (0, 1):
            for k, s in enumerate((1, -1)):
                self.recv(self.blkh(l, ab, -s, 1 - k), self.p2s.at[ab, 2 + k, j], self.p2r.at[ab, 2 + k, j])
                self.dd_send(self.blk(l, ab, -s), ab * 4 + 1 + k, j)
        for ab in (0, 1):
            for k in (0, 1):
                self.recv(self.blkh(l, ab, 2, k), self.p2s.at[ab, 4 + k, j], self.p2r.at[ab, 4 + k, j])
            self.dd_send(self.blk(l, ab, 2), ab * 4 + 3, j)
    def other(self):
        g = Gather.__new__(Gather)
        g.__dict__.update(self.__dict__)
        g.c = 1 - self.c
        return g
    def qkv_ready(self, j):
        g = self.other()
        l = self.stage_layer(j)
        for ab in (0, 1):
            for n, k in ((0, 0), (1, -1), (2, 1), (3, 2)):
                self.recv(g.blk(l, ab, k), self.ds.at[ab * 4 + n, j], self.dr.at[ab * 4 + n, j])

    def drain(self):
        for cp in self.pending:
            cp.wait_send()


def norm_into(x_ref, gain, h_ref, m):
    @pl.loop(0, m // 64)
    def _(i):
        r = pl.ds(pl.multiple_of(i * 64, 64), 64)
        v = x_ref[r, :].astype(F32)
        ms = jnp.mean(v * v, axis=-1, keepdims=True)
        h_ref[r, :] = (v * lax.rsqrt(ms + 1e-06) * gain).astype(BF)

def qkv_into(h_ref, w_ref, qkv_ref, m, tn=512):
    @pl.loop(0, 3072 // tn)
    def _(i):
        cidx = pl.ds(pl.multiple_of(i * tn, tn), tn)
        qkv_ref[pl.ds(0, m), cidx] = jnp.dot(h_ref[pl.ds(0, m), :], w_ref[:, cidx], preferred_element_type=F32).astype(BF)

def out_into(ctx_ref, w_ref, x_ref, y_ref, m, tn=256):
    @pl.loop(0, 1024 // tn)
    def _(i):
        cidx = pl.ds(pl.multiple_of(i * tn, tn), tn)
        u = jnp.dot(ctx_ref[pl.ds(0, m), :], w_ref[:, cidx], preferred_element_type=F32)
        y_ref[pl.ds(0, m), cidx] = (x_ref[pl.ds(0, m), cidx].astype(F32) + u).astype(BF)

def attend(q2, k2, v2, mask, lo, ind):
    z = jnp.zeros((), BF)
    kk = jnp.concatenate([jnp.where(lo, k2, z), jnp.where(lo, z, k2)], axis=0)
    vv = jnp.concatenate([jnp.where(lo, v2, z), jnp.where(lo, z, v2)], axis=0)
    vv = jnp.concatenate([vv, ind], axis=1)
    s = lax.dot_general(q2, kk, (((1,), (1,)), ((), ())), preferred_element_type=F32)
    if mask is not None:
        s = jnp.where(mask, s, -1e30)
    halves = []
    for n in (0, 1):
        t = s[:, n * 128:n * 128 + 128]
        t = jnp.exp2((t - jnp.max(t, axis=-1, keepdims=True)) * 0.18033688011112042)
        halves.append(t.astype(BF))
    o = jnp.dot(jnp.concatenate(halves, axis=1), vv, preferred_element_type=F32)
    return (o[:, :128] / o[:, 128:]).astype(BF)

def attention_into(kind, qkv_ref, ctx_ref, blocks, pairs=1):
    lo = lax.broadcasted_iota(jnp.int32, (128, 128), 1) < 64
    one, z = jnp.ones((), BF), jnp.zeros((), BF)
    ind = jnp.concatenate([jnp.where(lo, one, z), jnp.where(lo, z, one)], axis=0)
    i = lax.broadcasted_iota(jnp.int32, (128, 256), 0)
    j = lax.rem(lax.broadcasted_iota(jnp.int32, (128, 256), 1), 128)
    mask = None
    if kind == "frame":
        mask = lax.rem(i, 32) == lax.rem(j, 32)
    if kind == "row":
        mask = (lax.rem(i, 8) == lax.rem(j, 8)) & (i >= j)
    @pl.loop(0, HEADS // 2 // pairs)
    def _(step):
        for p in range(pairs):
            for b in range(blocks):
                first = (step * pairs + p) * 128

                def get(base):
                    c = pl.ds(pl.multiple_of(base + first, 128), 128)
                    if kind == "frame":
                        parts = [qkv_ref[pl.ds(f * 128 + b * 32, 32), c] for f in range(4)]
                        return jnp.concatenate(parts, axis=0)
                    return qkv_ref[pl.ds(b * 128, 128), c]

                o = attend(get(0), get(1024), get(2048), mask, lo, ind)
                c = pl.ds(pl.multiple_of(first, 128), 128)
                if kind == "frame":
                    for f in range(4):
                        ctx_ref[pl.ds(f * 128 + b * 32, 32), c] = o[f * 32 : f * 32 + 32]
                else:
                    ctx_ref[pl.ds(b * 128, 128), c] = o


def select_matrix(owner_row, owner_col, pick_ref):
    before = lax.broadcasted_iota(jnp.int32, (128, 128), 0) < lax.broadcasted_iota(jnp.int32, (128, 128), 1)
    alike = (owner_col == owner_row) & before
    slot = jnp.sum(jnp.where(alike, 1.0, 0.0), axis=0, keepdims=True)
    code = owner_row.astype(F32) * 8.0 + slot
    code = jnp.concatenate([code, code], axis=1)
    k = lax.broadcasted_iota(jnp.int32, (512, 256), 0)
    r = lax.broadcasted_iota(jnp.int32, (512, 256), 1)
    want = ((k // 16) * 8 + lax.rem(k, 8)).astype(F32)
    hit = (code == want) & (lax.rem(k // 8, 2) == r // 128)
    pick_ref[...] = jnp.where(hit, 1.0, 0.0).astype(BF)


def kernel(
    order, frames_in, owner_row, owner_col, wq_in, wo_in, g_in, out,
    wq, wo, g_all, frames, clip, pick, send, vol, h, qkv, *sems
):
    g = Gather(wq_in, wo_in, wq, wo, sems)
    g.barrier()
    g.start_x()
    own = g.own_copies(frames_in, frames, g_in, g_all)
    for cp in own:
        cp.start()
    g.gains_start(g_in, g_all)
    g.x_forward_qkv()
    g.wo_first()
    g.x_wait()
    g.p1s1(0)
    g.p1s1(1)
    select_matrix(owner_row[...], owner_col[...], pick)
    g.p1s2(0)
    g.p2s1(0)
    g.p1s2(1)
    own[0].wait()
    turn = order[3 - g.x]
    clip[...] = frames[turn].reshape(256, 1024)
    own[1].wait()
    g.gains_wait(g_all)
    norm_into(clip, g_all[0], h, 256)
    g.p2s2(0)
    g.wo_forward()
    g.p1s1(2)
    g.p2s1(1)
    g.fin(0)
    own[2].wait()
    own[3].wait()
    g.qkv_ready(0)
    qkv_into(h, wq.at[0], qkv, 256)
    g.p1s2(2)
    g.p2s2(1)
    attention_into("column", qkv, h, 2, 2)
    g.wo_ready(0)
    out_into(h, wo.at[0], clip, clip, 256)

    @pl.loop(0, 4)
    def _(i):
        c = pl.ds(pl.multiple_of(i * 256, 256), 256)
        send[:, c] = jnp.dot(pick[...], clip[:, c], preferred_element_type=F32).astype(BF)

    g.exchange_start(send, vol)
    g.p2s1(2)
    g.fin(1)
    g.qkv_ready(1)
    g.exchange_wait(send, vol)
    norm_into(vol, g_all[1], h, 512)
    qkv_into(h, wq.at[1], qkv, 512)
    g.p2s2(2)
    attention_into("frame", qkv, h, 4)
    g.wo_ready(1)
    out_into(h, wo.at[1], vol, vol, 512)
    g.fin(2)
    g.qkv_ready(2)
    g.wo_ready(2)
    g.wo_ready(3)
    for l in (2, 3):
        norm_into(vol, g_all[l], h, 512)
        qkv_into(h, wq.at[l], qkv, 512)
        attention_into("row", qkv, h, 4)
        out_into(h, wo.at[l], vol, out if l == 3 else vol, 512)
    g.exchange_drain(send, vol)
    g.drain()


def local(frames_in, order, owner, qkv_weight, out_weight, gains):
    vmem = pl.BlockSpec(memory_space=pltpu.VMEM)
    hbm = pl.BlockSpec(memory_space=pl.ANY)
    dma = pltpu.SemaphoreType.DMA
    result = pl.pallas_call(
        kernel,
        out_shape=jax.ShapeDtypeStruct((512, 1024), BF),
        in_specs=[pl.BlockSpec(memory_space=pltpu.SMEM), hbm, vmem, vmem, hbm, hbm, hbm],
        out_specs=vmem,
        scratch_shapes=[
            pltpu.VMEM((4, 1024, 3072), BF),
            pltpu.VMEM((4, 1024, 1024), BF),
            pltpu.VMEM((4, 1, 1024), F32),
            pltpu.VMEM((4, 2, 128, 1024), BF),
            pltpu.VMEM((256, 1024), BF),
            pltpu.VMEM((512, 256), BF),
            pltpu.VMEM((512, 1024), BF),
            pltpu.VMEM((512, 1024), BF),
            pltpu.VMEM((512, 1024), BF),
            pltpu.VMEM((512, 3072), BF),
            dma((4, 3)), dma((4, 3)),
            dma((2, 6, 3)), dma((2, 6, 3)),
            dma((2, 6, 3)), dma((2, 6, 3)),
            dma((10, 3)), dma((10, 3)),
            dma((3,)), dma((3,)),
            dma((32,)), dma((32,)),
            dma((4,)),
        ],
        compiler_params=pltpu.CompilerParams(
            collective_id=0, has_side_effects=True, vmem_limit_bytes=60 * 1024 * 1024
        ),
    )(order, frames_in, owner[None, :], owner[:, None], qkv_weight, out_weight, gains)
    return result.reshape(1, 64, 8, 1024)


def solution(mesh):
    placed = (
        P(None, "seq", None, None),
        P(),
        P(),
        P("section", None, None),
        P("section", None, None),
        P("section", None),
    )
    return jax.shard_map(
        local,
        mesh=mesh,
        in_specs=placed,
        out_specs=P("section", None, "seq", None),
        check_vma=False,
    )
```

profile of v0, /device:TPU:0, one launch (start us, length us, event | category | flops | bytes accessed | tf_op | source)
XLA Modules:
  0.0 121.8 jit_solution(13027735451723802393)
XLA Ops:
  0.0 1.4 %copy.7.owner_col = s32[128,1]{1,0:T(8,128)} copy(s32[128,1]{0,1:T(1,128)} %bitcast.4) | data formatting | bytes 1024 | tf_op jit(solution)/shard_map/broadcast_in_dim | solution.py:447
  1.4 118.1 %shard_map.64 = bf16[512,1024]{1,0:T(8,128)(2,1)} custom-call(s32[4]{0:T(128)} %order.1, bf16[4,2,128,1024]{3,2,1,0:T(8,128)(2,1)} %frames_in.1, s32[1,128]{1,0:T(1,128)} %bitcast.5, s32[128,1]{1,0:T(8,128)} %copy.7.owner_col, bf16[1,1024,3072]{2,1,0:T(8,128)(2,1)} %wq_in.1, bf16[1,1024,1024]{2,1,0:T(8,128)(2,1)} %wo_in.1, f32[1,1024]{1,0:T(1,128)} %g_in.1), custom_call_target="tpu_custom_call" | custom-call | tf_op jit(solution)/shard_map/pallas_call | solution.py:420
  119.5 2.3 %copy.9 = bf16[1,64,8,1024]{3,2,1,0:T(8,128)(2,1)} copy(bf16[1,64,8,1024]{3,2,1,0:T(8,128)(2,1)} %bitcast.3) | data formatting | bytes 2097152
where the time goes:
time: 123 us; the launch traced here: 122 us
  Pallas kernels  118 us (96%)
  local copies, waits for them, and re-layouts  3.65 us (3%)
    pallas_call x1, Pallas kernels, local(): pl.pallas_call(kernel, out_shape=jax.ShapeDtypeStruct((512, 1024), BF), i...  118 us

commit v1 on v0

--- a/solution.py
+++ b/solution.py
@@ -187,9 +187,15 @@
             l = self.layer_of(d)
             self.recv(self.sl(l, ab, 0), self.xs.at[ab, d - 1], self.xr.at[ab, d - 1])
             self.send(self.sl(l, ab, 0), self.sl(l, ab, 0), self.xs.at[ab, 1], self.xr.at[ab, 1], self.dev(dx=dx))
-    def x_wait(self):
-        for ab, d in ((0, 1), (1, 3), (0, 2), (1, 2)):
-            self.recv(self.sl(self.layer_of(d), ab, 0), self.xs.at[ab, d - 1], self.xr.at[ab, d - 1])
+    def slices_ready(self, j):
+        dist = lax.rem(self.stage_layer(j) - self.x + 4, 4)
+        for d, abs_ in ((1, (0,)), (2, (0, 1)), (3, (1,))):
+
+            @pl.when(dist == d)
+            def _():
+                for ab in abs_:
+                    self.recv(self.sl(self.layer_of(d), ab, 0), self.xs.at[ab, d - 1], self.xr.at[ab, d - 1])
+
     def dd_send(self, ref, a, b):
         self.send(ref, ref, self.ds.at[a, b], self.dr.at[a, b], self.dev(dc=1))
 
@@ -261,20 +267,20 @@
 
 
 def norm_into(x_ref, gain, h_ref, m):
-    @pl.loop(0, m // 64)
+    @pl.loop(0, m // 128)
     def _(i):
-        r = pl.ds(pl.multiple_of(i * 64, 64), 64)
+        r = pl.ds(pl.multiple_of(i * 128, 128), 128)
         v = x_ref[r, :].astype(F32)
         ms = jnp.mean(v * v, axis=-1, keepdims=True)
         h_ref[r, :] = (v * lax.rsqrt(ms + 1e-06) * gain).astype(BF)
 
-def qkv_into(h_ref, w_ref, qkv_ref, m, tn=512):
+def qkv_into(h_ref, w_ref, qkv_ref, m, tn=1024):
     @pl.loop(0, 3072 // tn)
     def _(i):
         cidx = pl.ds(pl.multiple_of(i * tn, tn), tn)
         qkv_ref[pl.ds(0, m), cidx] = jnp.dot(h_ref[pl.ds(0, m), :], w_ref[:, cidx], preferred_element_type=F32).astype(BF)
 
-def out_into(ctx_ref, w_ref, x_ref, y_ref, m, tn=256):
+def out_into(ctx_ref, w_ref, x_ref, y_ref, m, tn=512):
     @pl.loop(0, 1024 // tn)
     def _(i):
         cidx = pl.ds(pl.multiple_of(i * tn, tn), tn)
@@ -355,38 +361,40 @@
         cp.start()
     g.gains_start(g_in, g_all)
     g.x_forward_qkv()
+    g.slices_ready(0)
+    g.p1s1(0)
+    g.slices_ready(1)
+    g.p1s1(1)
     g.wo_first()
-    g.x_wait()
-    g.p1s1(0)
-    g.p1s1(1)
+    g.p1s2(0)
+    g.slices_ready(2)
+    g.p1s1(2)
+    g.p1s2(1)
+    g.p2s1(0)
     select_matrix(owner_row[...], owner_col[...], pick)
-    g.p1s2(0)
-    g.p2s1(0)
-    g.p1s2(1)
     own[0].wait()
     turn = order[3 - g.x]
     clip[...] = frames[turn].reshape(256, 1024)
+    g.p1s2(2)
     own[1].wait()
     g.gains_wait(g_all)
     norm_into(clip, g_all[0], h, 256)
     g.p2s2(0)
+    g.p2s1(1)
     g.wo_forward()
-    g.p1s1(2)
-    g.p2s1(1)
     g.fin(0)
     own[2].wait()
     own[3].wait()
     g.qkv_ready(0)
     qkv_into(h, wq.at[0], qkv, 256)
-    g.p1s2(2)
     g.p2s2(1)
-    attention_into("column", qkv, h, 2, 2)
+    attention_into("column", qkv, h, 2, 4)
     g.wo_ready(0)
     out_into(h, wo.at[0], clip, clip, 256)
 
-    @pl.loop(0, 4)
+    @pl.loop(0, 2)
     def _(i):
-        c = pl.ds(pl.multiple_of(i * 256, 256), 256)
+        c = pl.ds(pl.multiple_of(i * 512, 512), 512)
         send[:, c] = jnp.dot(pick[...], clip[:, c], preferred_element_type=F32).astype(BF)
 
     g.exchange_start(send, vol)
@@ -397,17 +405,17 @@
     norm_into(vol, g_all[1], h, 512)
     qkv_into(h, wq.at[1], qkv, 512)
     g.p2s2(2)
-    attention_into("frame", qkv, h, 4)
+    attention_into("frame", qkv, h, 4, 4)
     g.wo_ready(1)
     out_into(h, wo.at[1], vol, vol, 512)
     g.fin(2)
-    g.qkv_ready(2)
     g.wo_ready(2)
     g.wo_ready(3)
+    g.qkv_ready(2)
     for l in (2, 3):
         norm_into(vol, g_all[l], h, 512)
         qkv_into(h, wq.at[l], qkv, 512)
-        attention_into("row", qkv, h, 4)
+        attention_into("row", qkv, h, 4, 4)
         out_into(h, wo.at[l], vol, out if l == 3 else vol, 512)
     g.exchange_drain(send, vol)
     g.drain()

time: 123 us -> 110 us (0.89)
  Pallas kernels: 118 us -> 105 us
    pallas_call x1, Pallas kernels: 118 us -> 105 us  [local(): pl.pallas_call(kernel, out_shape=jax.ShapeDtypeStruct((512, 1024), BF), i...]
where the time goes in v1:
time: 110 us; the launch traced here: 108 us
  Pallas kernels  105 us (95%)
  local copies, waits for them, and re-layouts  3.65 us (3%)
    pallas_call x1, Pallas kernels, local(): pl.pallas_call(kernel, out_shape=jax.ShapeDtypeStruct((512, 1024), BF), i...  105 us
    unnamed x1, local copies, waits for them, and re-layouts  2.26 us

profile of v1, /device:TPU:0, one launch (start us, length us, event | category | flops | bytes accessed | tf_op | source)
XLA Modules:
  0.0 108.4 jit_solution(18003251110241400885)
XLA Ops:
  0.0 1.4 %copy.7.owner_col = s32[128,1]{1,0:T(8,128)} copy(s32[128,1]{0,1:T(1,128)} %bitcast.4) | data formatting | bytes 1024 | tf_op jit(solution)/shard_map/broadcast_in_dim | solution.py:455
  1.4 104.7 %shard_map.64 = bf16[512,1024]{1,0:T(8,128)(2,1)} custom-call(s32[4]{0:T(128)} %order.1, bf16[4,2,128,1024]{3,2,1,0:T(8,128)(2,1)} %frames_in.1, s32[1,128]{1,0:T(1,128)} %bitcast.5, s32[128,1]{1,0:T(8,128)} %copy.7.owner_col, bf16[1,1024,3072]{2,1,0:T(8,128)(2,1)} %wq_in.1, bf16[1,1024,1024]{2,1,0:T(8,128)(2,1)} %wo_in.1, f32[1,1024]{1,0:T(1,128)} %g_in.1), custom_call_target="tpu_custom_call" | custom-call | tf_op jit(solution)/shard_map/pallas_call | solution.py:428
  106.1 2.3 %copy.9 = bf16[1,64,8,1024]{3,2,1,0:T(8,128)(2,1)} copy(bf16[1,64,8,1024]{3,2,1,0:T(8,128)(2,1)} %bitcast.3) | data formatting | bytes 2097152

commit v2 on v1

--- a/solution.py
+++ b/solution.py
@@ -12,17 +12,44 @@
 F32, BF = jnp.float32, jnp.bfloat16
 
 
+class Lazy:
+    def __init__(self, ref):
+        self.ref, self.at = ref, self
+
+    def __getitem__(self, index):
+        return self.ref, index
+
+
+def view(sem):
+    return sem[0].at[sem[1]] if isinstance(sem, tuple) else sem
+
+
 class Gather:
     def __init__(self, wq_in, wo_in, wq, wo, sems):
         self.wq_in, self.wo_in, self.wq, self.wo = wq_in, wo_in, wq, wo
-        (self.xs, self.xr, self.p1s, self.p1r, self.p2s, self.p2r) = sems[:6]
-        (self.ds, self.dr, self.gs, self.gr, self.es, self.er, self.own) = sems[6:]
+        lazy = [Lazy(ref) for ref in sems[:10]]
+        (self.xs, self.xr, self.p1s, self.p1r, self.p2s, self.p2r) = lazy[:6]
+        (self.ds, self.dr, self.fs, self.fr) = lazy[6:]
+        (self.gs, self.gr, self.es, self.er, self.own) = sems[10:]
         self.x = lax.axis_index("section")
         self.q = lax.axis_index("seq")
         self.c = lax.rem(self.q, 2)
         self.y = lax.rem(self.q // 2, 4)
         self.z = self.q // 8
         self.pending = []
+        self.key = "all"
+        x = self.x
+        self.conds = {"x0": x == 0, "x1": x == 1, "x2": x == 2, "x3": x == 3}
+        self.conds |= {"own": x != 0, "d1": x != 3, "d2": x != 2, "d3": x != 1}
+
+    def when(self, key):
+        def run(f):
+            before = self.key
+            self.key = key if before == "all" else before + " " + key
+            pl.when(self.conds[key])(f)
+            self.key = before
+
+        return run
 
     def dev(self, dx=0, dy=0, dz=0, dc=0):
         x = lax.rem(self.x + (dx + 4), 4)
@@ -48,11 +75,17 @@
         pl.semaphore_wait(sem, 34)
 
     def copy(self, src, dst, ss, rs, dev):
-        return pltpu.make_async_remote_copy(src_ref=src, dst_ref=dst, send_sem=ss, recv_sem=rs, device_id=dev, device_id_type=MESH)
+        return pltpu.make_async_remote_copy(
+            src_ref=src, dst_ref=dst, send_sem=view(ss), recv_sem=view(rs), device_id=dev, device_id_type=MESH
+        )
+
     def send(self, src, dst, ss, rs, dev):
-        cp = self.copy(src, dst, ss, rs, dev)
-        cp.start()
-        self.pending.append(cp)
+        self.copy(src, dst, ss, rs, dev).start()
+        self.sent(src.shape, ss)
+
+    def sent(self, shape, ss, key=None):
+        self.pending.append((key or self.key, shape, ss))
+
     def recv(self, dst, ss, rs):
         self.copy(dst, dst, ss, rs, self.dev(dc=1)).wait_recv()
     def rows(self, ab, i=0, blk=0):
@@ -79,55 +112,41 @@
     def layer_of(self, d):
         return lax.rem(self.x + d, 4)
     def stage_layer(self, j):
-        return j + (self.x <= j).astype(jnp.int32)
+        return j + 1 + ((self.x > 0) & (self.x <= j + 1)).astype(jnp.int32)
     def start_x(self):
-        x = self.x
-        for ab in (0, 1):
-            a, b = self.rows(ab, 0)
-            src = self.wq_in.at[0, pl.ds(pl.multiple_of(a + b, 16), 16), :]
-            for dx, d in (((1, 3), (-1, 1)) if ab == 0 else ((-1, 1), (1, 3))):
-                self.send(src, self.sl(x, ab, 0), self.xs.at[ab, d - 1], self.xr.at[ab, d - 1], self.dev(dx=dx))
+        @self.when("own")
+        def _():
+            for ab in (0, 1):
+                a, b = self.rows(ab, 0)
+                src = self.wq_in.at[0, pl.ds(pl.multiple_of(a + b, 16), 16), :]
+                for dx, d in ((1, 3), (-1, 1)) if ab == 0 else ((-1, 1), (1, 3)):
+                    sems = self.xs.at[ab, d - 1], self.xr.at[ab, d - 1]
+                    self.send(src, self.sl(self.x, ab, 0), *sems, self.dev(dx=dx))
+
     def wo_own(self, second):
-        copies = []
-        for dx, d, h in ((1, 3, second), (-1, 1, 1 - second)):
-            src = self.wo_in.at[0, pl.ds(pl.multiple_of(self.c * 512 + h * 256, 256), 256), :]
-            sems = self.xs.at[2 + h, d - 1], self.xr.at[2 + h, d - 1]
-            copies.append(self.copy(src, self.wop(self.x, h), *sems, self.dev(dx=dx)))
-        return copies
-
-    def wo_first(self):
-        for cp in self.wo_own(0):
-            cp.start()
-            self.pending.append(cp)
-        second = self.wo_own(1)
-        self.pending.extend(second)
-
-        @pl.when(self.x == 0)
+        @self.when("own")
         def _():
-            for cp in second:
-                cp.start()
+            for dx, d, h in ((1, 3, second), (-1, 1, 1 - second)):
+                src = self.wo_in.at[0, pl.ds(pl.multiple_of(self.c * 512 + h * 256, 256), 256), :]
+                sems = self.xs.at[2 + h, d - 1], self.xr.at[2 + h, d - 1]
+                self.send(src, self.wop(self.x, h), *sems, self.dev(dx=dx))
 
     def wo_forward(self):
         for h, d, dx in ((0, 3, 1), (1, 1, -1)):
-            r = self.wop(self.layer_of(d), h)
-            self.recv(r, self.xs.at[2 + h, d - 1], self.xr.at[2 + h, d - 1])
-            self.send(r, r, self.xs.at[2 + h, 1], self.xr.at[2 + h, 1], self.dev(dx=dx))
-            self.dd_send(r, 8 + h, d - 1)
-
-        @pl.when(self.x != 0)
-        def _():
-            for cp in self.wo_own(1):
-                cp.start()
+
+            @self.when(f"d{d}")
+            def _():
+                r = self.wop(self.layer_of(d), h)
+                self.recv(r, self.xs.at[2 + h, d - 1], self.xr.at[2 + h, d - 1])
+                self.send(r, r, self.xs.at[2 + h, 1], self.xr.at[2 + h, 1], self.dev(dx=dx))
+                self.dd_send(r, 8 + h, d - 1)
 
     def wo_ready(self, layer):
         dist = lax.rem(layer - self.x + 4, 4)
         for d, hs in ((1, (0,)), (2, (0, 1)), (3, (1,))):
-            if layer == 0:
+            if layer == 1:
                 for h in hs:
-                    r = self.wop(self.layer_of(d), h)
-                    self.pending.append(
-                        self.copy(r, r, self.ds.at[8 + h, d - 1], self.dr.at[8 + h, d - 1], self.dev(dc=1))
-                    )
+                    self.sent((256, 1024), self.ds.at[8 + h, d - 1], f"d{d}")
 
             @pl.when(dist == d)
             def _():
@@ -139,13 +158,45 @@
                 for h in (0, 1):
                     self.recv(g.wop(self.layer_of(d), h), self.ds.at[8 + h, d - 1], self.dr.at[8 + h, d - 1])
 
-    def gains_start(self, g_in, g_all):
-        for dx in (1, 2, 3):
-            self.send(g_in, g_all.at[self.x], self.gs.at[dx - 1], self.gr.at[dx - 1], self.dev(dx=dx))
+    def gains_copies(self, g_in, g_all):
+        dst = g_all.at[self.x]
+        return [
+            self.copy(g_in, dst, self.gs.at[dx - 1], self.gr.at[dx - 1], self.dev(dx=dx)) for dx in (1, 2, 3)
+        ]
 
     def gains_wait(self, g_all):
         for dx in (1, 2, 3):
             self.recv(g_all.at[self.layer_of(4 - dx)], self.gs.at[dx - 1], self.gr.at[dx - 1])
+
+    def columns_send(self, x1, t):
+        if t == 2:
+            for n, dx in ((0, 1), (1, -1)):
+                r = x1.at[2, pl.ds(n * 128, 128), :]
+                self.send(r, r, self.fs.at[2 + n], self.fr.at[2 + n], self.dev(dx=dx))
+        else:
+            n, dx = (0, 1) if t == 1 else (1, -1)
+            self.send(x1.at[t], x1.at[t], self.fs.at[n], self.fr.at[n], self.dev(dx=dx))
+
+    def columns_relay(self, x1):
+        for n, dx, key in ((0, 1, "x1"), (1, -1, "x3")):
+
+            @self.when(key)
+            def _():
+                r = x1.at[2, pl.ds(n * 128, 128), :]
+                self.recv(r, self.fs.at[2 + n], self.fr.at[2 + n])
+                self.send(r, r, self.fs.at[4 + n], self.fr.at[4 + n], self.dev(dx=dx))
+
+    def columns_wait(self, x1):
+        for n, key, t in ((0, "x1", 1), (1, "x3", 3)):
+
+            @self.when(key)
+            def _():
+                self.recv(x1.at[t], self.fs.at[n], self.fr.at[n])
+
+        @self.when("x2")
+        def _():
+            for n in (0, 1):
+                self.recv(x1.at[2, pl.ds(n * 128, 128), :], self.fs.at[4 + n], self.fr.at[4 + n])
 
     def exchange_copy(self, k, send, land):
         src = send.at[pl.ds(pl.multiple_of(self.peer(k)[1] * 16, 16), 16), :]
@@ -184,9 +235,13 @@
 
     def x_forward_qkv(self):
         for ab, d, dx in ((0, 3, 1), (1, 1, -1)):
-            l = self.layer_of(d)
-            self.recv(self.sl(l, ab, 0), self.xs.at[ab, d - 1], self.xr.at[ab, d - 1])
-            self.send(self.sl(l, ab, 0), self.sl(l, ab, 0), self.xs.at[ab, 1], self.xr.at[ab, 1], self.dev(dx=dx))
+
+            @self.when(f"d{d}")
+            def _():
+                r = self.sl(self.layer_of(d), ab, 0)
+                self.recv(r, self.xs.at[ab, d - 1], self.xr.at[ab, d - 1])
+                self.send(r, r, self.xs.at[ab, 1], self.xr.at[ab, 1], self.dev(dx=dx))
+
     def slices_ready(self, j):
         dist = lax.rem(self.stage_layer(j) - self.x + 4, 4)
         for d, abs_ in ((1, (0,)), (2, (0, 1)), (3, (1,))):
@@ -262,8 +317,18 @@
                 self.recv(g.blk(l, ab, k), self.ds.at[ab * 4 + n, j], self.dr.at[ab * 4 + n, j])
 
     def drain(self):
-        for cp in self.pending:
-            cp.wait_send()
+        def wait(items):
+            for shape, ss in items:
+                r = self.wq.at[0, pl.ds(0, shape[0]), pl.ds(0, shape[1])]
+                self.copy(r, r, ss, self.dr.at[0, 0], self.dev(dc=1)).wait_send()
+
+        for key in dict.fromkeys(k for k, _, _ in self.pending):
+            items = [(shape, ss) for k, shape, ss in self.pending if k == key]
+            if key == "all":
+                wait(items)
+            else:
+                met = functools.reduce(jnp.logical_and, [self.conds[k] for k in key.split()])
+                pl.when(met)(functools.partial(wait, items))
 
 
 def norm_into(x_ref, gain, h_ref, m):
@@ -351,72 +416,129 @@
 
 def kernel(
     order, frames_in, owner_row, owner_col, wq_in, wo_in, g_in, out,
-    wq, wo, g_all, frames, clip, pick, send, vol, h, qkv, *sems
+    wq, wo, g_all, frames, x1, pick, send, vol, h, qkv, *sems
 ):
     g = Gather(wq_in, wo_in, wq, wo, sems)
+
+    def columns_first(t):
+        x1[t] = frames[order[3 - t]].reshape(256, 1024)
+        norm_into(x1.at[t], g_all[0], h, 256)
+        qkv_into(h, wq.at[0], qkv, 256)
+
+    def columns_rest(t):
+        attention_into("column", qkv, h, 2, 4)
+        out_into(h, wo.at[0], x1.at[t], x1.at[t], 256)
+
+    def exchange_start():
+        @pl.loop(0, 2)
+        def _(i):
+            c = pl.ds(pl.multiple_of(i * 512, 512), 512)
+            send[:, c] = jnp.dot(pick[...], x1[g.x, :, c], preferred_element_type=F32).astype(BF)
+
+        g.exchange_start(send, vol)
+
+    def at0(*steps):
+        @g.when("x0")
+        def _():
+            for step in steps:
+                step()
+
+    part = functools.partial
     g.barrier()
     g.start_x()
     own = g.own_copies(frames_in, frames, g_in, g_all)
     for cp in own:
         cp.start()
-    g.gains_start(g_in, g_all)
-    g.x_forward_qkv()
-    g.slices_ready(0)
-    g.p1s1(0)
-    g.slices_ready(1)
-    g.p1s1(1)
-    g.wo_first()
-    g.p1s2(0)
-    g.slices_ready(2)
-    g.p1s1(2)
-    g.p1s2(1)
-    g.p2s1(0)
+    gains = g.gains_copies(g_in, g_all)
+    for cp in gains:
+        cp.start()
     select_matrix(owner_row[...], owner_col[...], pick)
-    own[0].wait()
-    turn = order[3 - g.x]
-    clip[...] = frames[turn].reshape(256, 1024)
-    g.p1s2(2)
-    own[1].wait()
+    for cp in own:
+        cp.wait()
+
+    def send_columns(t):
+        columns_rest(t)
+        g.columns_send(x1, t)
+
+    at0(
+        part(columns_first, 2),
+        g.x_forward_qkv,
+        part(g.slices_ready, 0),
+        part(g.p1s1, 0),
+        part(send_columns, 2),
+        part(g.slices_ready, 1),
+        part(g.p1s1, 1),
+        part(g.p1s2, 0),
+        part(columns_first, 3),
+        part(g.slices_ready, 2),
+        part(g.p1s1, 2),
+        part(g.p1s2, 1),
+        part(send_columns, 3),
+        part(g.p2s1, 0),
+        part(columns_first, 1),
+        part(g.p1s2, 2),
+        part(send_columns, 1),
+        part(g.p2s1, 1),
+        part(columns_first, 0),
+        part(g.p2s2, 0),
+        part(columns_rest, 0),
+        exchange_start,
+        g.wo_forward,
+        part(g.fin, 0),
+        part(g.p2s2, 1),
+        part(g.p2s1, 2),
+    )
+
+    @g.when("own")
+    def _():
+        g.x_forward_qkv()
+        g.slices_ready(0)
+        g.p1s1(0)
+        g.slices_ready(1)
+        g.p1s1(1)
+        g.wo_own(0)
+        g.p1s2(0)
+        g.p1s2(1)
+        g.p2s1(0)
+        g.columns_relay(x1)
+        g.p2s2(0)
+        g.wo_forward()
+        g.wo_own(1)
+        g.columns_wait(x1)
+        exchange_start()
+        g.p2s1(1)
+        g.fin(0)
+
+    def own_do(step, j):
+        g.when("own")(part(step, j))
+
     g.gains_wait(g_all)
-    norm_into(clip, g_all[0], h, 256)
-    g.p2s2(0)
-    g.p2s1(1)
-    g.wo_forward()
-    g.fin(0)
-    own[2].wait()
-    own[3].wait()
-    g.qkv_ready(0)
-    qkv_into(h, wq.at[0], qkv, 256)
-    g.p2s2(1)
-    attention_into("column", qkv, h, 2, 4)
-    g.wo_ready(0)
-    out_into(h, wo.at[0], clip, clip, 256)
-
-    @pl.loop(0, 2)
-    def _(i):
-        c = pl.ds(pl.multiple_of(i * 512, 512), 512)
-        send[:, c] = jnp.dot(pick[...], clip[:, c], preferred_element_type=F32).astype(BF)
-
-    g.exchange_start(send, vol)
-    g.p2s1(2)
-    g.fin(1)
-    g.qkv_ready(1)
     g.exchange_wait(send, vol)
     norm_into(vol, g_all[1], h, 512)
+    g.qkv_ready(0)
     qkv_into(h, wq.at[1], qkv, 512)
-    g.p2s2(2)
+    own_do(g.p2s2, 1)
+    at0(part(g.fin, 1))
     attention_into("frame", qkv, h, 4, 4)
+    at0(part(g.p2s2, 2))
     g.wo_ready(1)
     out_into(h, wo.at[1], vol, vol, 512)
-    g.fin(2)
+    own_do(g.fin, 1)
+    norm_into(vol, g_all[2], h, 512)
+    g.qkv_ready(1)
+    qkv_into(h, wq.at[2], qkv, 512)
+    attention_into("row", qkv, h, 4, 4)
     g.wo_ready(2)
+    out_into(h, wo.at[2], vol, vol, 512)
+    at0(part(g.fin, 2))
+    norm_into(vol, g_all[3], h, 512)
+    at0(part(g.qkv_ready, 2))
     g.wo_ready(3)
-    g.qkv_ready(2)
-    for l in (2, 3):
-        norm_into(vol, g_all[l], h, 512)
-        qkv_into(h, wq.at[l], qkv, 512)
-        attention_into("row", qkv, h, 4, 4)
-        out_into(h, wo.at[l], vol, out if l == 3 else vol, 512)
+    qkv_into(h, wq.at[3], qkv, 512)
+    attention_into("row", qkv, h, 4, 4)
+    out_into(h, wo.at[3], vol, out, 512)
+    for cp in gains:
+        cp.wait_send()
     g.exchange_drain(send, vol)
     g.drain()
 
@@ -435,7 +557,7 @@
             pltpu.VMEM((4, 1024, 1024), BF),
             pltpu.VMEM((4, 1, 1024), F32),
             pltpu.VMEM((4, 2, 128, 1024), BF),
-            pltpu.VMEM((256, 1024), BF),
+            pltpu.VMEM((4, 256, 1024), BF),
             pltpu.VMEM((512, 256), BF),
             pltpu.VMEM((512, 1024), BF),
             pltpu.VMEM((512, 1024), BF),
@@ -445,6 +567,7 @@
             dma((2, 6, 3)), dma((2, 6, 3)),
             dma((2, 6, 3)), dma((2, 6, 3)),
             dma((10, 3)), dma((10, 3)),
+            dma((6,)), dma((6,)),
             dma((3,)), dma((3,)),
             dma((32,)), dma((32,)),
             dma((4,)),

time: 110 us -> 106 us (0.964)
  Pallas kernels: 105 us -> 101 us
    pallas_call x1, Pallas kernels: 105 us -> 101 us  [local(): pl.pallas_call(kernel, out_shape=jax.ShapeDtypeStruct((512, 1024), BF), i...]
where the time goes in v2:
time: 106 us; the launch traced here: 105 us
  Pallas kernels  101 us (95%)
  local copies, waits for them, and re-layouts  3.65 us (3%)
    pallas_call x1, Pallas kernels, local(): pl.pallas_call(kernel, out_shape=jax.ShapeDtypeStruct((512, 1024), BF), i...  101 us
    unnamed x1, local copies, waits for them, and re-layouts  2.26 us

profile of v2, /device:TPU:0, one launch (start us, length us, event | category | flops | bytes accessed | tf_op | source)
XLA Modules:
  0.0 105.0 jit_solution(15257153747909806196)
XLA Ops:
  0.0 1.4 %copy.7.owner_col = s32[128,1]{1,0:T(8,128)} copy(s32[128,1]{0,1:T(1,128)} %bitcast.4) | data formatting | bytes 1024 | tf_op jit(solution)/shard_map/broadcast_in_dim | solution.py:578
  1.4 101.3 %shard_map.64 = bf16[512,1024]{1,0:T(8,128)(2,1)} custom-call(s32[4]{0:T(128)} %order.1, bf16[4,2,128,1024]{3,2,1,0:T(8,128)(2,1)} %frames_in.1, s32[1,128]{1,0:T(1,128)} %bitcast.5, s32[128,1]{1,0:T(8,128)} %copy.7.owner_col, bf16[1,1024,3072]{2,1,0:T(8,128)(2,1)} %wq_in.1, bf16[1,1024,1024]{2,1,0:T(8,128)(2,1)} %wo_in.1, f32[1,1024]{1,0:T(1,128)} %g_in.1), custom_call_target="tpu_custom_call" | custom-call | tf_op jit(solution)/shard_map/pallas_call | solution.py:550
  102.7 2.3 %copy.9 = bf16[1,64,8,1024]{3,2,1,0:T(8,128)(2,1)} copy(bf16[1,64,8,1024]{3,2,1,0:T(8,128)(2,1)} %bitcast.3) | data formatting | bytes 2097152

commit v3 on v2

--- a/solution.py
+++ b/solution.py
@@ -63,7 +63,7 @@
     def source(self, k):
         return self.dev(0, 4 - lax.rem(k // 2, 4), 4 - k // 8, 2 - lax.rem(k, 2))[1]
 
-    def barrier(self):
+    def greet(self):
         sem = pltpu.get_barrier_semaphore()
         for dx in (1, 2, 3):
             pl.semaphore_signal(sem, inc=1, device_id=self.dev(dx=dx), device_id_type=MESH)
@@ -72,7 +72,8 @@
         def _(k):
             pl.semaphore_signal(sem, inc=1, device_id=self.peer(k), device_id_type=MESH)
 
-        pl.semaphore_wait(sem, 34)
+    def greeted(self):
+        pl.semaphore_wait(pltpu.get_barrier_semaphore(), 34)
 
     def copy(self, src, dst, ss, rs, dev):
         return pltpu.make_async_remote_copy(
@@ -332,20 +333,20 @@
 
 
 def norm_into(x_ref, gain, h_ref, m):
-    @pl.loop(0, m // 128)
+    @pl.loop(0, m // 256)
     def _(i):
-        r = pl.ds(pl.multiple_of(i * 128, 128), 128)
+        r = pl.ds(pl.multiple_of(i * 256, 256), 256)
         v = x_ref[r, :].astype(F32)
         ms = jnp.mean(v * v, axis=-1, keepdims=True)
         h_ref[r, :] = (v * lax.rsqrt(ms + 1e-06) * gain).astype(BF)
 
-def qkv_into(h_ref, w_ref, qkv_ref, m, tn=1024):
+def qkv_into(h_ref, w_ref, qkv_ref, m, tn=3072):
     @pl.loop(0, 3072 // tn)
     def _(i):
         cidx = pl.ds(pl.multiple_of(i * tn, tn), tn)
         qkv_ref[pl.ds(0, m), cidx] = jnp.dot(h_ref[pl.ds(0, m), :], w_ref[:, cidx], preferred_element_type=F32).astype(BF)
 
-def out_into(ctx_ref, w_ref, x_ref, y_ref, m, tn=512):
+def out_into(ctx_ref, w_ref, x_ref, y_ref, m, tn=1024):
     @pl.loop(0, 1024 // tn)
     def _(i):
         cidx = pl.ds(pl.multiple_of(i * tn, tn), tn)
@@ -444,17 +445,17 @@
                 step()
 
     part = functools.partial
-    g.barrier()
-    g.start_x()
+    g.greet()
     own = g.own_copies(frames_in, frames, g_in, g_all)
     for cp in own:
         cp.start()
+    select_matrix(owner_row[...], owner_col[...], pick)
+    g.greeted()
+    g.start_x()
     gains = g.gains_copies(g_in, g_all)
     for cp in gains:
         cp.start()
-    select_matrix(owner_row[...], owner_col[...], pick)
-    for cp in own:
-        cp.wait()
+    at0(*(cp.wait for cp in own))
 
     def send_columns(t):
         columns_rest(t)
@@ -512,6 +513,11 @@
     def own_do(step, j):
         g.when("own")(part(step, j))
 
+    @g.when("own")
+    def _():
+        for cp in own:
+            cp.wait()
+
     g.gains_wait(g_all)
     g.exchange_wait(send, vol)
     norm_into(vol, g_all[1], h, 512)
@@ -519,7 +525,7 @@
     qkv_into(h, wq.at[1], qkv, 512)
     own_do(g.p2s2, 1)
     at0(part(g.fin, 1))
-    attention_into("frame", qkv, h, 4, 4)
+    attention_into("frame", qkv, h, 4, 8)
     at0(part(g.p2s2, 2))
     g.wo_ready(1)
     out_into(h, wo.at[1], vol, vol, 512)
@@ -527,7 +533,7 @@
     norm_into(vol, g_all[2], h, 512)
     g.qkv_ready(1)
     qkv_into(h, wq.at[2], qkv, 512)
-    attention_into("row", qkv, h, 4, 4)
+    attention_into("row", qkv, h, 4, 8)
     g.wo_ready(2)
     out_into(h, wo.at[2], vol, vol, 512)
     at0(part(g.fin, 2))
@@ -535,7 +541,7 @@
     at0(part(g.qkv_ready, 2))
     g.wo_ready(3)
     qkv_into(h, wq.at[3], qkv, 512)
-    attention_into("row", qkv, h, 4, 4)
+    attention_into("row", qkv, h, 4, 8)
     out_into(h, wo.at[3], vol, out, 512)
     for cp in gains:
         cp.wait_send()

time: 106 us -> 103 us (0.972)
  Pallas kernels: 101 us -> 98.5 us
    pallas_call x1, Pallas kernels: 101 us -> 98.5 us  [local(): pl.pallas_call(kernel, out_shape=jax.ShapeDtypeStruct((512, 1024), BF), i...]
where the time goes in v3:
time: 103 us; the launch traced here: 102 us
  Pallas kernels  98.5 us (96%)
  local copies, waits for them, and re-layouts  3.65 us (4%)
    pallas_call x1, Pallas kernels, local(): pl.pallas_call(kernel, out_shape=jax.ShapeDtypeStruct((512, 1024), BF), i...  98.5 us
    unnamed x1, local copies, waits for them, and re-layouts  2.26 us

profile of v3, /device:TPU:0, one launch (start us, length us, event | category | flops | bytes accessed | tf_op | source)
XLA Modules:
  0.0 102.1 jit_solution(9528694638483133836)
XLA Ops:
  0.0 1.4 %copy.7.owner_col = s32[128,1]{1,0:T(8,128)} copy(s32[128,1]{0,1:T(1,128)} %bitcast.4) | data formatting | bytes 1024 | tf_op jit(solution)/shard_map/broadcast_in_dim | solution.py:584
  1.4 98.5 %shard_map.64 = bf16[512,1024]{1,0:T(8,128)(2,1)} custom-call(s32[4]{0:T(128)} %order.1, bf16[4,2,128,1024]{3,2,1,0:T(8,128)(2,1)} %frames_in.1, s32[1,128]{1,0:T(1,128)} %bitcast.5, s32[128,1]{1,0:T(8,128)} %copy.7.owner_col, bf16[1,1024,3072]{2,1,0:T(8,128)(2,1)} %wq_in.1, bf16[1,1024,1024]{2,1,0:T(8,128)(2,1)} %wo_in.1, f32[1,1024]{1,0:T(1,128)} %g_in.1), custom_call_target="tpu_custom_call" | custom-call | tf_op jit(solution)/shard_map/pallas_call | solution.py:556
  99.9 2.3 %copy.9 = bf16[1,64,8,1024]{3,2,1,0:T(8,128)(2,1)} copy(bf16[1,64,8,1024]{3,2,1,0:T(8,128)(2,1)} %bitcast.3) | data formatting | bytes 2097152
